TPU v7x, 32 devices: a whole 2x2x4 slice. The times are simulated.
32 devices in a mesh: ice: 2 (over core), lat: 4 (over y, x), lon: 4 (over z).
Axes of the slice: x: 2, y: 2, z: 4, core: 2. Of those that a mesh axis runs over, the one named last changes fastest.
Arguments:
- adjoint_final: float32 [2, 4, 24, 128, 512], P('ice', None, None, 'lat', 'lon'), may hold values from -6 to 6
- land_mask: int32 [128, 512], P('lat', 'lon'), may hold values 0 or 1
- coupling_depth: int32 [2, 128, 512], P('ice', 'lat', 'lon'), may hold values from 1 to 24
- coupling_weight: float32 [2, 4, 128, 512], P('ice', None, 'lat', 'lon'), may hold values from 0.2 to 0.8
- diffusion: float32 [2, 2, 24, 128, 512], P(None, 'ice', None, 'lat', 'lon'), may hold values from 0.02 to 0.12
- velocity: float32 [2, 2, 2, 24, 128, 512], P(None, 'ice', None, None, 'lat', 'lon'), may hold values from -0.15 to 0.15
- mixing: float32 [2, 2, 24, 128, 512], P(None, 'ice', None, 'lat', 'lon'), may hold values from 0.05 to 0.3
Outputs:
- adjoint_start: float32 [2, 4, 24, 128, 512], P('ice', None, None, 'lat', 'lon')
All inputs are finite; a program needn't handle non-finite values. No bound on the sum of `land_mask` on one device may be relied on, other than what follows from the above.
Results may differ from a plain program's by a relative error of at most 0.00002.
Values sent between devices are 32-bit elements; how exact they have to be, the bound alone decides.
A program may use at most 128 MiB of HBM per device.

v0:
```python
import jax
import jax.numpy as jnp
from jax import lax
from jax.sharding import PartitionSpec as P

STEPS = 2


def padded(cells, sides, width, closed):
    for axis, dim in sides:
        count = lax.axis_size(axis)
        ends = count if closed else count - 1
        head = lax.slice_in_dim(cells, 0, width, axis=dim)
        tail = lax.slice_in_dim(cells, cells.shape[dim] - width, cells.shape[dim], axis=dim)
        cells = jnp.concatenate(
            [
                lax.ppermute(tail, axis, [(i, (i + 1) % count) for i in range(ends)]),
                cells,
                lax.ppermute(head, axis, [((i + 1) % count, i) for i in range(ends)]),
            ],
            axis=dim,
        )
    return cells


def swapped(block, axis, apart):
    count = lax.axis_size(axis)
    route = []
    for low in range(count):
        high = low | 1 << apart
        if high != low and high < count:
            route += [(low, high), (high, low)]
    return lax.ppermute(block, axis, route)


def adjoint_transport(adjoint, land_cells, spread, zonal, merid, vertical, fold_sign, top_row):
    masked = land_cells * adjoint
    diff_part = spread * masked
    zonal_part = zonal * masked
    merid_part = merid * masked
    vert_part = vertical * masked
    result = masked - 4.0 * diff_part - 2.0 * vert_part
    blank_level = jnp.zeros_like(vert_part[:, :, :1])
    result = result + jnp.concatenate([blank_level, vert_part[:, :, :-1]], axis=2)
    result = result + jnp.concatenate([vert_part[:, :, 1:], blank_level], axis=2)
    stacked_parts = jnp.stack([diff_part, zonal_part, merid_part])
    zonal_halo = padded(stacked_parts, (("lon", 5),), 1, True)
    merid_halo = padded(stacked_parts, (("lat", 4),), 1, False)
    from_west = zonal_halo[0, ..., :-2] - zonal_halo[1, ..., :-2]
    from_east = zonal_halo[0, ..., 2:] + zonal_halo[1, ..., 2:]
    from_south = merid_halo[0, ..., :-2, :] - merid_halo[2, ..., :-2, :]
    from_north = merid_halo[0, ..., 2:, :] + merid_halo[2, ..., 2:, :]
    result = result + from_west + from_east + from_south + from_north
    fold_row = diff_part[..., -1, :] - merid_part[..., -1, :]
    bit_total = lax.axis_size("lon").bit_length() - 1
    mirror = fold_row
    for bit_index in range(bit_total):
        mirror = swapped(mirror, "lon", bit_index)
    mirror = mirror[..., ::-1]
    fold_term = jnp.where(top_row, fold_sign * mirror, 0.0)
    return result.at[..., -1, :].add(fold_term)


def shards(adjoint_final, land_mask, coupling_depth, coupling_weight, diffusion, velocity, mixing):
    levels = adjoint_final.shape[2]
    land_cells = land_mask.astype(jnp.float32)
    level_index = lax.broadcasted_iota(jnp.int32, (1, levels, 1, 1), 1)
    depth_cells = coupling_depth[:, None, :, :]
    profile = jnp.where(level_index < depth_cells, 1.0, 0.0).astype(
        jnp.float32
    ) / depth_cells.astype(jnp.float32)
    fold_sign = jnp.array([1.0, 1.0, -1.0, -1.0], jnp.float32)[None, :, None, None]
    top_row = lax.axis_index("lat") == lax.axis_size("lat") - 1
    adjoint = adjoint_final
    for moment in reversed(range(STEPS)):
        shares = coupling_weight * jnp.sum(profile[:, None] * adjoint, axis=2)
        partner_flux = swapped(shares, "ice", 0)
        adjoint = adjoint.at[:, :, 0].add(partner_flux - shares)
        adjoint = adjoint_transport(
            adjoint,
            land_cells,
            diffusion[moment][:, None],
            velocity[moment][:, 0][:, None],
            velocity[moment][:, 1][:, None],
            mixing[moment][:, None],
            fold_sign,
            top_row,
        )
    return adjoint


def solution(mesh):
    in_specs = (
        P("ice", None, None, "lat", "lon"),
        P("lat", "lon"),
        P("ice", "lat", "lon"),
        P("ice", None, "lat", "lon"),
        P(None, "ice", None, "lat", "lon"),
        P(None, "ice", None, None, "lat", "lon"),
        P(None, "ice", None, "lat", "lon"),
    )
    out_specs = P("ice", None, None, "lat", "lon")
    return jax.shard_map(shards, mesh=mesh, in_specs=in_specs, out_specs=out_specs, check_vma=False)
```

profile of v0, /device:TPU:12, one launch (start us, length us, event | category | flops | bytes accessed | tf_op | source)
XLA Modules:
  0.0 149.0 jit_solution(15644746516533749275)
XLA Ops:
  1.5 2.8 %multiply_reduce_fusion.1 = (f32[4,32,128]{2,0,1:T(4,128)S(1)}, f32[1,4,24,32,128]{4,2,1,3,0:T(8,128)S(1)}) fusion(f32[24,32,128]{2,0,1:T(8,128)S(1)} %select_divide_fusion, f32[1,4,24,32,128]{4,3,2,1,0:T(8,128)} %param.16), kind=kLoop, calls=%fused_computation.47 | loop fusion | flops 770048 | bytes 3604480 | tf_op jit(solution)/shard_map/reduce_sum | solution.py:76
  6.0 1.0 slice_bitcast_fusion.3
  8.4 1.0 copy.98
  9.4 1.0 copy.100
  10.4 1.0 copy.99
  13.2 1.3 scatter-add.14
  14.5 3.8 %multiply_multiply_fusion.5 = (f32[1,4,24,32,128]{4,2,1,3,0:T(8,128)S(1)}, f32[1,1,4,24,32,128]{5,3,2,4,1,0:T(8,128)S(1)}, f32[1,4,24,32,128]{4,2,1,3,0:T(8,128)...) fusion(f32[1,4,24,32,128]{4,2,1,3,0:T(8,128)S(1)} %scatter-add.14, f32[24,32,128]{2,0,1:T(8,128)S(1)} %copy.97, ...), kind=kLoop, calls=%fused_computation.53 | loop fusion | flops 1966080 | bytes 11026432 | tf_op jit(solution)/shard_map/mul | solution.py:38
  21.6 3.4 %collective-permute-start.3 = (f32[3,1,4,24,1,128]{5,3,2,4,1,0:T(8,128)}, f32[3,1,4,24,1,128]{5,3,2,4,1,0:T(8,128)}, u32[]{:S(2)}, u32[]{:S(2)}) collective-permute-start(f32[3,1,4,24,1,128]{5,3,2,4,1,0:T(8,128)} %get-tuple-element.57), channel_id=1, source_target_pairs={{0,4},{4,8},{8,12},{1,5},{5,9},{9,13},{2,6},{6,10},{10,14},{3,7},{... | collective-permute-start | bytes 442376 | tf_op jit(solution)/shard_map/ppermute | solution.py:17
  25.0 3.3 %collective-permute-start.4 = (f32[3,1,4,24,1,128]{5,3,2,4,1,0:T(8,128)}, f32[3,1,4,24,1,128]{5,3,2,4,1,0:T(8,128)}, u32[]{:S(2)}, u32[]{:S(2)}) collective-permute-start(f32[3,1,4,24,1,128]{5,3,2,4,1,0:T(8,128)} %get-tuple-element.58), channel_id=1, source_target_pairs={{4,0},{8,4},{12,8},{5,1},{9,5},{13,9},{6,2},{10,6},{14,10},{7,3},{... | collective-permute-start | bytes 442376 | tf_op jit(solution)/shard_map/ppermute | solution.py:19
  28.3 5.3 %fusion.29 = (f32[3,1,4,24,32,1]{5,3,2,4,1,0:T(8,128)}, f32[3,1,4,24,32,1]{5,3,2,4,1,0:T(8,128)}) fusion(f32[3,1,4,24,32,128]{5,3,2,4,1,0:T(8,128)S(1)} %pad_maximum_fusion), kind=kLoop, calls=%fused_computation.86 | loop fusion | bytes 147456 | tf_op jit(solution)/shard_map/slice | solution.py:14
  33.6 4.2 %copy.101 = f32[3,1,4,24,32,1]{4,3,5,2,1,0:T(8,128)} copy(f32[3,1,4,24,32,1]{5,3,2,4,1,0:T(8,128)} %get-tuple-element.55) | data formatting | bytes 73728 | tf_op jit(solution)/shard_map/slice | solution.py:14
  37.7 4.3 %copy.103 = f32[3,1,4,24,32,1]{4,3,5,2,1,0:T(8,128)} copy(f32[3,1,4,24,32,1]{5,3,2,4,1,0:T(8,128)} %get-tuple-element.56) | data formatting | bytes 73728 | tf_op jit(solution)/shard_map/slice | solution.py:13
  42.0 1.6 %collective-permute-start.2 = (f32[3,1,4,24,32,1]{4,3,5,2,1,0:T(8,128)}, f32[3,1,4,24,32,1]{4,3,5,2,1,0:T(8,128)}, u32[]{:S(2)}, u32[]{:S(2)}) collective-permute-start(f32[3,1,4,24,32,1]{4,3,5,2,1,0:T(8,128)} %copy.103), channel_id=1, source_target_pairs={{1,0},{2,1},{3,2},{0,3},{5,4},{6,5},{7,6},{4,7},{9,8},{10,9},{11,1... | collective-permute-start | bytes 110600 | tf_op jit(solution)/shard_map/ppermute | solution.py:19
  43.6 1.1 collective-permute-start.1
  44.7 3.7 %collective-permute-start.6 = (f32[1,4,24,128]{3,2,1,0:T(8,128)}, f32[1,4,24,128]{3,2,1,0:T(8,128)}, u32[]{:S(2)}, u32[]{:S(2)}) collective-permute-start(f32[1,4,24,128]{3,2,1,0:T(8,128)} %collective-permute-done.5), channel_id=1, source_target_pairs={{0,2},{2,0},{1,3},{3,1},{4,6},{6,4},{5,7},{7,5},{8,10},{10,8},{9,1... | collective-permute-start | bytes 147464 | tf_op jit(solution)/shard_map/ppermute | solution.py:33
  48.4 2.1 %fusion.31 = (f32[1,4,23,32,128]{4,2,1,3,0:T(8,128)}, f32[1,4,23,32,128]{4,2,1,3,0:T(8,128)}) fusion(f32[1,4,24,32,128]{4,2,1,3,0:T(8,128)S(1)} %copy-done.11), kind=kLoop, calls=%fused_computation.88 | loop fusion | bytes 6029312 | tf_op jit(solution)/shard_map/slice | solution.py:44
  50.5 3.0 %collective-permute-done.1 = f32[3,1,4,24,32,1]{4,3,5,2,1,0:T(8,128)} collective-permute-done((f32[3,1,4,24,32,1]{4,3,5,2,1,0:T(8,128)}, f32[3,1,4,24,32,1]{4,3,5,2,1,0:T(8,128)}, u32[]{:S(2)}, u32[]{:S(2)}) %collective-permute-start.1) | collective-permute-done | bytes 36896 | tf_op jit(solution)/shard_map/ppermute | solution.py:17
  53.5 4.2 %copy.102 = f32[3,1,4,24,32,1]{5,3,2,4,1,0:T(8,128)} copy(f32[3,1,4,24,32,1]{4,3,5,2,1,0:T(8,128)} %collective-permute-done.1) | data formatting | bytes 73728 | tf_op jit(solution)/shard_map/ppermute | solution.py:17
  57.8 4.3 %copy.104 = f32[3,1,4,24,32,1]{5,3,2,4,1,0:T(8,128)} copy(f32[3,1,4,24,32,1]{4,3,5,2,1,0:T(8,128)} %collective-permute-done.2) | data formatting | bytes 73728 | tf_op jit(solution)/shard_map/ppermute | solution.py:19
  62.0 1.5 %rev.6 = f32[1,4,24,128]{3,2,1,0:T(8,128)} reverse(f32[1,4,24,128]{3,2,1,0:T(8,128)} %collective-permute-done.6), dimensions={3} | reverse | bytes 98304 | tf_op jit(solution)/shard_map/rev | solution.py:59
  63.5 9.7 %fusion.13 = f32[1,4,24,32,128]{4,2,1,3,0:T(8,128)S(1)} fusion(f32[3,1,4,24,1,128]{5,3,2,4,1,0:T(8,128)} %collective-permute-done.4, f32[1,1,4,24,32,128]{5,3,2,4,1,0:T(8,128)S(1)} %bitcast.94, f32[1,1,4,24,32,128]{5,3,2,4,1,0:T(8,128)} %copy-done.3, f32[1,1,4,24,32,128]{5,3,2,4,1,0:T(8,128)} %copy-done.2, ...), kind=kLoop, calls=%fused_computation.22 | loop fusion | flops 16121856 | bytes 12050432 | tf_op jit(solution)/shard_map/add | solution.py:53
  73.3 1.0 fusion.25
  74.3 1.4 multiply_reduce_fusion
  77.2 1.6 %scatter-add.16 = f32[1,4,24,32,128]{4,2,1,3,0:T(8,128)S(1)} dynamic-update-slice(f32[1,4,24,32,128]{4,2,1,3,0:T(8,128)S(1)} %fusion.25, f32[1,4,1,32,128]{4,2,1,3,0:T(1,128)S(1)} %slice_add_fusion, s32[]{:T(128)} %constant.106.clone.1, s32[]{:T(128)} %constant.106.clone.1, s32[]{:T(128)} %constant.106.clone.1, s32[]{:T(128)} %constant.106.clone.1, s32[]{:T(128)} %constant.106.clone.1) | dynamic-update-slice | bytes 131076 | tf_op jit(solution)/shard_map/scatter-add | solution.py:78
  78.8 2.2 %multiply_multiply_fusion.2 = (f32[1,4,24,32,128]{4,2,1,3,0:T(8,128)S(1)}, f32[1,1,4,24,32,128]{5,3,2,4,1,0:T(8,128)S(1)}, f32[1,4,24,32,128]{4,2,1,3,0:T(8,128)...) fusion(f32[1,4,24,32,128]{4,2,1,3,0:T(8,128)S(1)} %scatter-add.16, f32[24,32,128]{2,0,1:T(8,128)S(1)} %copy.106, ...), kind=kLoop, calls=%fused_computation.50 | loop fusion | flops 1966080 | bytes 11026432 | tf_op jit(solution)/shard_map/mul | solution.py:38
  80.9 0.9 copy.131
  82.5 1.5 %collective-permute-start.12 = (f32[1,4,24,128]{3,2,1,0:T(8,128)}, f32[1,4,24,128]{3,2,1,0:T(8,128)}, u32[]{:S(2)}, u32[]{:S(2)}) collective-permute-start(f32[1,4,24,128]{3,2,1,0:T(8,128)} %fusion.23), channel_id=1, source_target_pairs={{0,1},{1,0},{2,3},{3,2},{4,5},{5,4},{6,7},{7,6},{8,9},{9,8},{10,11... | collective-permute-start | bytes 147464 | tf_op jit(solution)/shard_map/ppermute | solution.py:33
  84.0 0.9 copy.111
  84.9 0.9 copy.112
  87.3 5.3 %fusion.28 = (f32[3,1,4,24,32,1]{5,4,3,2,1,0:T(8,128)}, f32[3,1,4,24,32,1]{5,4,3,2,1,0:T(8,128)}) fusion(f32[3,1,4,24,32,128]{5,4,3,2,1,0:T(8,128)S(1)} %pad_maximum_fusion.1), kind=kLoop, calls=%fused_computation.85 | loop fusion | bytes 147456 | tf_op jit(solution)/shard_map/slice | solution.py:14
  92.5 4.1 %copy.113 = f32[3,1,4,24,32,1]{4,3,5,2,1,0:T(8,128)} copy(f32[3,1,4,24,32,1]{5,4,3,2,1,0:T(8,128)} %get-tuple-element.53) | data formatting | bytes 73728 | tf_op jit(solution)/shard_map/slice | solution.py:14
  96.7 4.1 %copy.116 = f32[3,1,4,24,32,1]{4,3,5,2,1,0:T(8,128)} copy(f32[3,1,4,24,32,1]{5,4,3,2,1,0:T(8,128)} %get-tuple-element.54) | data formatting | bytes 73728 | tf_op jit(solution)/shard_map/slice | solution.py:13
  101.3 1.5 %collective-permute-start.8 = (f32[3,1,4,24,32,1]{4,3,5,2,1,0:T(8,128)}, f32[3,1,4,24,32,1]{4,3,5,2,1,0:T(8,128)}, u32[]{:S(2)}, u32[]{:S(2)}) collective-permute-start(f32[3,1,4,24,32,1]{4,3,5,2,1,0:T(8,128)} %copy.113), channel_id=1, source_target_pairs={{0,1},{1,2},{2,3},{3,0},{4,5},{5,6},{6,7},{7,4},{8,9},{9,10},{10,1... | collective-permute-start | bytes 110600 | tf_op jit(solution)/shard_map/ppermute | solution.py:17
  102.8 2.9 %collective-permute-start.13 = (f32[1,4,24,128]{3,2,1,0:T(8,128)}, f32[1,4,24,128]{3,2,1,0:T(8,128)}, u32[]{:S(2)}, u32[]{:S(2)}) collective-permute-start(f32[1,4,24,128]{3,2,1,0:T(8,128)} %collective-permute-done.12), channel_id=1, source_target_pairs={{0,2},{2,0},{1,3},{3,1},{4,6},{6,4},{5,7},{7,5},{8,10},{10,8},{9,1... | collective-permute-start | bytes 147464 | tf_op jit(solution)/shard_map/ppermute | solution.py:33
  105.7 4.1 %fusion.30 = (f32[1,4,23,32,128]{4,2,1,3,0:T(8,128)}, f32[1,4,23,32,128]{4,2,1,3,0:T(8,128)}) fusion(f32[1,4,24,32,128]{4,2,1,3,0:T(8,128)} %get-tuple-element.63), kind=kLoop, calls=%fused_computation.87 | loop fusion | bytes 6029312 | tf_op jit(solution)/shard_map/slice | solution.py:44
  110.6 2.7 %copy.115 = f32[3,1,4,24,32,128]{5,3,2,4,1,0:T(8,128)S(1)} copy(f32[3,1,4,24,32,128]{5,4,3,2,1,0:T(8,128)S(1)} %copy-done.1) | data formatting | bytes 9437184 | tf_op jit(solution)/shard_map/stack | solution.py:46
  113.3 3.1 %collective-permute-start.11 = (f32[3,1,4,24,1,128]{5,4,3,2,1,0:T(1,128)}, f32[3,1,4,24,1,128]{5,4,3,2,1,0:T(1,128)}, u32[]{:S(2)}, u32[]{:S(2)}) collective-permute-start(f32[3,1,4,24,1,128]{5,4,3,2,1,0:T(1,128)} %slice.337), channel_id=1, source_target_pairs={{4,0},{8,4},{12,8},{5,1},{9,5},{13,9},{6,2},{10,6},{14,10},{7,3},{... | collective-permute-start | bytes 442376 | tf_op jit(solution)/shard_map/ppermute | solution.py:19
  117.1 3.4 %collective-permute-start.10 = (f32[3,1,4,24,1,128]{5,3,2,4,1,0:T(8,128)}, f32[3,1,4,24,1,128]{5,3,2,4,1,0:T(8,128)}, u32[]{:S(2)}, u32[]{:S(2)}) collective-permute-start(f32[3,1,4,24,1,128]{5,3,2,4,1,0:T(8,128)} %slice.334), channel_id=1, source_target_pairs={{0,4},{4,8},{8,12},{1,5},{5,9},{9,13},{2,6},{6,10},{10,14},{3,7},{... | collective-permute-start | bytes 442376 | tf_op jit(solution)/shard_map/ppermute | solution.py:17
  120.5 4.5 %copy.114 = f32[3,1,4,24,32,1]{5,3,2,4,1,0:T(8,128)} copy(f32[3,1,4,24,32,1]{4,3,5,2,1,0:T(8,128)} %collective-permute-done.8) | data formatting | bytes 73728 | tf_op jit(solution)/shard_map/ppermute | solution.py:17
  125.0 4.3 %copy.118 = f32[3,1,4,24,32,1]{5,3,2,4,1,0:T(8,128)} copy(f32[3,1,4,24,32,1]{4,3,5,2,1,0:T(8,128)} %collective-permute-done.9) | data formatting | bytes 73728 | tf_op jit(solution)/shard_map/ppermute | solution.py:19
  129.3 1.5 %rev.7 = f32[1,4,24,128]{3,2,1,0:T(8,128)} reverse(f32[1,4,24,128]{3,2,1,0:T(8,128)} %collective-permute-done.13), dimensions={3} | reverse | bytes 98304 | tf_op jit(solution)/shard_map/rev | solution.py:59
  130.8 0.9 multiply_select_fusion
  131.7 1.1 constant_dynamic-update-slice_fusion.1
  132.8 5.3 %constant_dynamic-update-slice_fusion = f32[3,1,4,24,33,128]{5,3,2,4,1,0:T(8,128)S(1)} fusion(f32[3,1,4,24,33,128]{5,3,2,4,1,0:T(8,128)S(1)} %constant_dynamic-update-slice_fusion.1, f32[3,1,4,24,32,128]{5,4,3,2,1,0:T(8,128)} %copy-done), kind=kLoop, calls=%fused_computation.82 | loop fusion | bytes 9437184 | tf_op jit(solution)/shard_map/concatenate | solution.py:15
  138.2 4.7 %fusion.4 = f32[1,4,24,32,128]{4,2,1,3,0:T(8,128)S(1)} fusion(f32[3,1,4,24,33,128]{5,3,2,4,1,0:T(8,128)S(1)} %constant_dynamic-update-slice_fusion, f32[3,1,4,24,32,1]{5,3,2,4,1,0:T(8,128)} %copy.118, f32[3,1,4,24,32,128]{5,3,2,4,1,0:T(8,128)S(1)} %bitcast.96, f32[3,1,4,24,32,1]{5,3,2,4,1,0:T(8,128)S(1)} %copy-done.5, ...), kind=kLoop, calls=%fused_computation.10 | loop fusion | flops 7471104 | bytes 14901248 | tf_op jit(solution)/shard_map/add | solution.py:53
  143.0 2.1 %fusion.2 = f32[1,4,24,32,128]{4,3,2,1,0:T(8,128)S(1)} fusion(f32[3,1,4,24,1,128]{5,4,3,2,1,0:T(1,128)} %collective-permute-done.11, f32[1,1,4,24,32,128]{5,4,3,2,1,0:T(8,128)S(1)} %bitcast.98, f32[1,1,4,24,32,128]{5,4,3,2,1,0:T(8,128)S(1)} %copy-done.10, f32[1,1,4,24,32,128]{5,4,3,2,1,0:T(8,128)S(1)} %copy-done.8, f32[1,4,24,32,128]{4,2,1,3,0:T(8,128)S(1)} %fusion.4), kind=kLoop, calls=%fused_computation.5 | loop fusion | flops 3145728 | bytes 8011776 | tf_op jit(solution)/shard_map/add | solution.py:53
  145.2 1.1 copy-done.15
  146.3 2.7 %scatter-add.19 = f32[1,4,24,32,128]{4,3,2,1,0:T(8,128)} dynamic-update-slice(f32[1,4,24,32,128]{4,3,2,1,0:T(8,128)} %copy-done.15, f32[1,4,24,1,128]{4,3,2,1,0:T(1,128)S(1)} %slice_add_fusion.1, s32[]{:T(128)} %constant.106.clone.1, s32[]{:T(128)} %constant.106.clone.1, s32[]{:T(128)} %constant.106.clone.1, s32[]{:T(128)} %constant.112.clone.1, s32[]{:T(128)} %constant.106.clone.1) | dynamic-update-slice | bytes 98308 | tf_op jit(solution)/shard_map/scatter-add | solution.py:61
  (99 shorter events, 15.2 us)
Async XLA Ops:
  1.5 2.8 %copy-start.12 = (f32[24,32,128]{2,0,1:T(8,128)}, f32[24,32,128]{2,0,1:T(8,128)S(1)}, u32[]{:S(2)}) copy-start(f32[24,32,128]{2,0,1:T(8,128)S(1)} %select_divide_fusion) | copy-start | bytes 1179652
  1.5 2.8 %copy-start.23 = (f32[1,4,32,128]{3,2,1,0:T(8,128)S(1)}, f32[1,4,32,128]{3,2,1,0:T(8,128)}, u32[]{:S(2)}) copy-start(f32[1,4,32,128]{3,2,1,0:T(8,128)} %param.19) | copy-start | bytes 196612
  1.5 3.5 %copy-start.21 = (f32[2,1,24,32,128]{4,3,2,1,0:T(8,128)S(1)}, f32[2,1,24,32,128]{4,3,2,1,0:T(8,128)}, u32[]{:S(2)}) copy-start(f32[2,1,24,32,128]{4,3,2,1,0:T(8,128)} %param.20) | copy-start | bytes 2359300
  4.3 1.5 %copy-start.16 = (f32[2,1,2,24,32,128]{5,4,3,2,1,0:T(8,128)S(1)}, f32[2,1,2,24,32,128]{5,4,3,2,1,0:T(8,128)}, u32[]{:S(2)}) copy-start(f32[2,1,2,24,32,128]{5,4,3,2,1,0:T(8,128)} %param.21) | copy-start | bytes 4718596
  5.0 6.3 %collective-permute-start = (f32[1,4,32,128]{3,1,2,0:T(4,128)}, f32[1,4,32,128]{3,1,2,0:T(4,128)}, u32[]{:S(2)}, u32[]{:S(2)}) collective-permute-start(f32[1,4,32,128]{3,1,2,0:T(4,128)} %bitcast_multiply_fusion.1), channel_id=1, source_target_pairs={{0,16},{16,0},{1,17},{17,1},{2,18},{18,2},{3,19},{19,3},{4,20},{20... | collective-permute-start | bytes 196616 | tf_op jit(solution)/shard_map/ppermute | solution.py:33
  6.0 1.3 copy-start.22
  7.3 0.8 copy-start.25
  14.5 3.8 %copy-start.6 = (f32[1,4,24,32,128]{4,2,1,3,0:T(8,128)}, f32[1,4,24,32,128]{4,2,1,3,0:T(8,128)S(1)}, u32[]{:S(2)}) copy-start(f32[1,4,24,32,128]{4,2,1,3,0:T(8,128)S(1)} %scatter-add.14) | copy-start | bytes 4718596
  18.3 1.2 copy-start.2
  18.3 1.8 %copy-start.3 = (f32[1,1,4,24,32,128]{5,3,2,4,1,0:T(8,128)}, f32[1,1,4,24,32,128]{5,3,2,4,1,0:T(8,128)S(1)}, u32[]{:S(2)}) copy-start(f32[1,1,4,24,32,128]{5,3,2,4,1,0:T(8,128)S(1)} %get-tuple-element.67) | copy-start | bytes 4718596
  21.1 23.6 %collective-permute-start.5 = (f32[1,4,24,128]{3,2,1,0:T(8,128)}, f32[1,4,24,128]{3,2,1,0:T(8,128)}, u32[]{:S(2)}, u32[]{:S(2)}) collective-permute-start(f32[1,4,24,128]{3,2,1,0:T(8,128)} %fusion.24), channel_id=1, source_target_pairs={{0,1},{1,0},{2,3},{3,2},{4,5},{5,4},{6,7},{7,6},{8,9},{9,8},{10,11... | collective-permute-start | bytes 147464 | tf_op jit(solution)/shard_map/ppermute | solution.py:33
  21.6 42.0 %collective-permute-start.3 = (f32[3,1,4,24,1,128]{5,3,2,4,1,0:T(8,128)}, f32[3,1,4,24,1,128]{5,3,2,4,1,0:T(8,128)}, u32[]{:S(2)}, u32[]{:S(2)}) collective-permute-start(f32[3,1,4,24,1,128]{5,3,2,4,1,0:T(8,128)} %get-tuple-element.57), channel_id=1, source_target_pairs={{0,4},{4,8},{8,12},{1,5},{5,9},{9,13},{2,6},{6,10},{10,14},{3,7},{... | collective-permute-start | bytes 442376 | tf_op jit(solution)/shard_map/ppermute | solution.py:17
  25.0 38.6 %collective-permute-start.4 = (f32[3,1,4,24,1,128]{5,3,2,4,1,0:T(8,128)}, f32[3,1,4,24,1,128]{5,3,2,4,1,0:T(8,128)}, u32[]{:S(2)}, u32[]{:S(2)}) collective-permute-start(f32[3,1,4,24,1,128]{5,3,2,4,1,0:T(8,128)} %get-tuple-element.58), channel_id=1, source_target_pairs={{4,0},{8,4},{12,8},{5,1},{9,5},{13,9},{6,2},{10,6},{14,10},{7,3},{... | collective-permute-start | bytes 442376 | tf_op jit(solution)/shard_map/ppermute | solution.py:19
  37.7 10.7 %copy-start.11 = (f32[1,4,24,32,128]{4,2,1,3,0:T(8,128)S(1)}, f32[1,4,24,32,128]{4,2,1,3,0:T(8,128)}, u32[]{:S(2)}) copy-start(f32[1,4,24,32,128]{4,2,1,3,0:T(8,128)} %get-tuple-element.66) | copy-start | bytes 4718596
  42.0 15.7 %collective-permute-start.2 = (f32[3,1,4,24,32,1]{4,3,5,2,1,0:T(8,128)}, f32[3,1,4,24,32,1]{4,3,5,2,1,0:T(8,128)}, u32[]{:S(2)}, u32[]{:S(2)}) collective-permute-start(f32[3,1,4,24,32,1]{4,3,5,2,1,0:T(8,128)} %copy.103), channel_id=1, source_target_pairs={{1,0},{2,1},{3,2},{0,3},{5,4},{6,5},{7,6},{4,7},{9,8},{10,9},{11,1... | collective-permute-start | bytes 110600 | tf_op jit(solution)/shard_map/ppermute | solution.py:19
  43.6 9.9 %collective-permute-start.1 = (f32[3,1,4,24,32,1]{4,3,5,2,1,0:T(8,128)}, f32[3,1,4,24,32,1]{4,3,5,2,1,0:T(8,128)}, u32[]{:S(2)}, u32[]{:S(2)}) collective-permute-start(f32[3,1,4,24,32,1]{4,3,5,2,1,0:T(8,128)} %copy.101), channel_id=1, source_target_pairs={{0,1},{1,2},{2,3},{3,0},{4,5},{5,6},{6,7},{7,4},{8,9},{9,10},{10,1... | collective-permute-start | bytes 110600 | tf_op jit(solution)/shard_map/ppermute | solution.py:17
  44.7 17.3 %collective-permute-start.6 = (f32[1,4,24,128]{3,2,1,0:T(8,128)}, f32[1,4,24,128]{3,2,1,0:T(8,128)}, u32[]{:S(2)}, u32[]{:S(2)}) collective-permute-start(f32[1,4,24,128]{3,2,1,0:T(8,128)} %collective-permute-done.5), channel_id=1, source_target_pairs={{0,2},{2,0},{1,3},{3,1},{4,6},{6,4},{5,7},{7,5},{8,10},{10,8},{9,1... | collective-permute-start | bytes 147464 | tf_op jit(solution)/shard_map/ppermute | solution.py:33
  73.3 2.4 %copy-start.24 = (f32[1,4,32,128]{3,2,1,0:T(8,128)S(1)}, f32[1,4,32,128]{3,2,1,0:T(8,128)}, u32[]{:S(2)}) copy-start(f32[1,4,32,128]{3,2,1,0:T(8,128)} %param.19) | copy-start | bytes 196612
  73.3 2.6 %copy-start.19 = (f32[24,32,128]{2,1,0:T(8,128)S(1)}, f32[24,32,128]{2,1,0:T(8,128)}, u32[]{:S(2)}) copy-start(f32[24,32,128]{2,1,0:T(8,128)} %get-tuple-element.79) | copy-start | bytes 1179652
  73.3 2.8 %copy-start.20 = (f32[24,32,128]{2,1,0:T(8,128)S(1)}, f32[24,32,128]{2,1,0:T(8,128)}, u32[]{:S(2)}) copy-start(f32[24,32,128]{2,1,0:T(8,128)} %get-tuple-element.77) | copy-start | bytes 1179652
  74.3 2.1 %copy-start.18 = (f32[24,32,128]{2,1,0:T(8,128)S(1)}, f32[24,32,128]{2,1,0:T(8,128)}, u32[]{:S(2)}) copy-start(f32[24,32,128]{2,1,0:T(8,128)} %get-tuple-element.81) | copy-start | bytes 1179652
  75.7 1.0 copy-start.17
  75.8 1.3 collective-permute-start.7
  76.4 4.6 %copy-start.13 = (f32[24,32,128]{2,0,1:T(8,128)}, f32[24,32,128]{2,0,1:T(8,128)S(1)}, u32[]{:S(2)}) copy-start(f32[24,32,128]{2,0,1:T(8,128)S(1)} %copy.107) | copy-start | bytes 1179652
  82.5 20.3 %collective-permute-start.12 = (f32[1,4,24,128]{3,2,1,0:T(8,128)}, f32[1,4,24,128]{3,2,1,0:T(8,128)}, u32[]{:S(2)}, u32[]{:S(2)}) collective-permute-start(f32[1,4,24,128]{3,2,1,0:T(8,128)} %fusion.23), channel_id=1, source_target_pairs={{0,1},{1,0},{2,3},{3,2},{4,5},{5,4},{6,7},{7,6},{8,9},{9,8},{10,11... | collective-permute-start | bytes 147464 | tf_op jit(solution)/shard_map/ppermute | solution.py:33
  84.9 1.2 copy-start.7
  85.9 1.4 copy-start.9
  87.3 5.3 %copy-start = (f32[3,1,4,24,32,128]{5,4,3,2,1,0:T(8,128)}, f32[3,1,4,24,32,128]{5,4,3,2,1,0:T(8,128)S(1)}, u32[]{:S(2)}) copy-start(f32[3,1,4,24,32,128]{5,4,3,2,1,0:T(8,128)S(1)} %pad_maximum_fusion.1) | copy-start | bytes 14155780
  100.8 24.2 %collective-permute-start.9 = (f32[3,1,4,24,32,1]{4,3,5,2,1,0:T(8,128)}, f32[3,1,4,24,32,1]{4,3,5,2,1,0:T(8,128)}, u32[]{:S(2)}, u32[]{:S(2)}) collective-permute-start(f32[3,1,4,24,32,1]{4,3,5,2,1,0:T(8,128)} %copy.116), channel_id=1, source_target_pairs={{1,0},{2,1},{3,2},{0,3},{5,4},{6,5},{7,6},{4,7},{9,8},{10,9},{11,1... | collective-permute-start | bytes 110600 | tf_op jit(solution)/shard_map/ppermute | solution.py:19
  101.3 19.3 %collective-permute-start.8 = (f32[3,1,4,24,32,1]{4,3,5,2,1,0:T(8,128)}, f32[3,1,4,24,32,1]{4,3,5,2,1,0:T(8,128)}, u32[]{:S(2)}, u32[]{:S(2)}) collective-permute-start(f32[3,1,4,24,32,1]{4,3,5,2,1,0:T(8,128)} %copy.113), channel_id=1, source_target_pairs={{0,1},{1,2},{2,3},{3,0},{4,5},{5,6},{6,7},{7,4},{8,9},{9,10},{10,1... | collective-permute-start | bytes 110600 | tf_op jit(solution)/shard_map/ppermute | solution.py:17
  102.8 26.5 %collective-permute-start.13 = (f32[1,4,24,128]{3,2,1,0:T(8,128)}, f32[1,4,24,128]{3,2,1,0:T(8,128)}, u32[]{:S(2)}, u32[]{:S(2)}) collective-permute-start(f32[1,4,24,128]{3,2,1,0:T(8,128)} %collective-permute-done.12), channel_id=1, source_target_pairs={{0,2},{2,0},{1,3},{3,1},{4,6},{6,4},{5,7},{7,5},{8,10},{10,8},{9,1... | collective-permute-start | bytes 147464 | tf_op jit(solution)/shard_map/ppermute | solution.py:33
  105.7 4.1 %copy-start.1 = (f32[3,1,4,24,32,128]{5,4,3,2,1,0:T(8,128)S(1)}, f32[3,1,4,24,32,128]{5,4,3,2,1,0:T(8,128)}, u32[]{:S(2)}) copy-start(f32[3,1,4,24,32,128]{5,4,3,2,1,0:T(8,128)} %copy-done) | copy-start | bytes 14155780
  113.3 3.1 %copy-start.4 = (f32[3,1,4,24,32,128]{5,3,2,4,1,0:T(8,128)}, f32[3,1,4,24,32,128]{5,3,2,4,1,0:T(8,128)S(1)}, u32[]{:S(2)}) copy-start(f32[3,1,4,24,32,128]{5,3,2,4,1,0:T(8,128)S(1)} %copy.115) | copy-start | bytes 14155780
  113.3 29.6 %collective-permute-start.11 = (f32[3,1,4,24,1,128]{5,4,3,2,1,0:T(1,128)}, f32[3,1,4,24,1,128]{5,4,3,2,1,0:T(1,128)}, u32[]{:S(2)}, u32[]{:S(2)}) collective-permute-start(f32[3,1,4,24,1,128]{5,4,3,2,1,0:T(1,128)} %slice.337), channel_id=1, source_target_pairs={{4,0},{8,4},{12,8},{5,1},{9,5},{13,9},{6,2},{10,6},{14,10},{7,3},{... | collective-permute-start | bytes 442376 | tf_op jit(solution)/shard_map/ppermute | solution.py:19
  117.1 14.6 %collective-permute-start.10 = (f32[3,1,4,24,1,128]{5,3,2,4,1,0:T(8,128)}, f32[3,1,4,24,1,128]{5,3,2,4,1,0:T(8,128)}, u32[]{:S(2)}, u32[]{:S(2)}) collective-permute-start(f32[3,1,4,24,1,128]{5,3,2,4,1,0:T(8,128)} %slice.334), channel_id=1, source_target_pairs={{0,4},{4,8},{8,12},{1,5},{5,9},{9,13},{2,6},{6,10},{10,14},{3,7},{... | collective-permute-start | bytes 442376 | tf_op jit(solution)/shard_map/ppermute | solution.py:17
  130.8 7.4 %copy-start.14 = (f32[24,32,128]{2,0,1:T(8,128)S(1)}, f32[24,32,128]{2,0,1:T(8,128)}, u32[]{:S(2)}) copy-start(f32[24,32,128]{2,0,1:T(8,128)} %copy-done.13) | copy-start | bytes 1179652
  131.7 6.4 %slice-start = ((s8[4718592]{0:T(1024)(128)(4,1)}), s8[4194304]{0:T(1024)(128)(4,1)S(1)}, s32[]{:S(2)}) async-start(s8[4718592]{0:T(1024)(128)(4,1)} %bitcast.95), calls=%async_computation | async-start | bytes 8388608
  132.8 5.4 %slice-start.1 = ((s8[4718592]{0:T(1024)(128)(4,1)}), s8[524288]{0:T(1024)(128)(4,1)S(1)}, s32[]{:S(2)}) async-start(s8[4718592]{0:T(1024)(128)(4,1)} %bitcast.95), calls=%async_computation.1 | async-start | bytes 1048576
  132.8 5.4 %copy-start.5 = (f32[3,1,4,24,32,1]{5,3,2,4,1,0:T(8,128)S(1)}, f32[3,1,4,24,32,1]{5,3,2,4,1,0:T(8,128)}, u32[]{:S(2)}) copy-start(f32[3,1,4,24,32,1]{5,3,2,4,1,0:T(8,128)} %copy.114) | copy-start | bytes 110596
  138.2 4.8 %copy-start.8 = (f32[1,1,4,24,32,128]{5,4,3,2,1,0:T(8,128)S(1)}, f32[1,1,4,24,32,128]{5,4,3,2,1,0:T(8,128)}, u32[]{:S(2)}) copy-start(f32[1,1,4,24,32,128]{5,4,3,2,1,0:T(8,128)} %copy-done.7) | copy-start | bytes 4718596
  138.2 4.8 %copy-start.10 = (f32[1,1,4,24,32,128]{5,4,3,2,1,0:T(8,128)S(1)}, f32[1,1,4,24,32,128]{5,4,3,2,1,0:T(8,128)}, u32[]{:S(2)}) copy-start(f32[1,1,4,24,32,128]{5,4,3,2,1,0:T(8,128)} %copy-done.9) | copy-start | bytes 4718596
  145.1 1.1 copy-start.15
where the time goes:
time: 150 us; the launch traced here: 149 us
  local copies, waits for them, and re-layouts  83.1 us (55%)
  other arithmetic  35.6 us (24%)
  starting transfers between devices  26.6 us (18%)
  waiting for transfers between devices  3.21 us (2%)
    slice x5, local copies, waits for them, and re-layouts, padded(): lax.slice_in_dim(cells, cells.shape[dim] - width, cells.shape[dim], axis=...  19.5 us
    add x3, other arithmetic, adjoint_transport(): result = result + from_west + from_east + from_south + from_north  16.6 us
    ppermute x4, starting transfers between devices, padded(): lax.ppermute(tail, axis, [(i, (i + 1) % count) for i in range(ends)])  9.45 us
    slice x3, local copies, waits for them, and re-layouts, padded(): head = lax.slice_in_dim(cells, 0, width, axis=dim)  9.2 us
    ppermute x2, local copies, waits for them, and re-layouts, padded(): lax.ppermute(tail, axis, [(i, (i + 1) % count) for i in range(ends)])  8.69 us
    ppermute x6, starting transfers between devices, swapped(): return lax.ppermute(block, axis, route)  8.65 us
    ppermute x2, local copies, waits for them, and re-layouts, padded(): lax.ppermute(head, axis, [((i + 1) % count, i) for i in range(ends)])  8.6 us
    ppermute x4, starting transfers between devices, padded(): lax.ppermute(head, axis, [((i + 1) % count, i) for i in range(ends)])  8.49 us
  transfers between devices with their start and end apart: 14, of which 2 were waited for; matrix products, arithmetic and copies ran while one was open for 53% of the time, Pallas kernels for 0%

commit v1 on v0

v1 whole, which is shorter than its diff:
```python
import functools

import jax
import jax.numpy as jnp
from jax import lax
from jax.experimental import pallas as pl
from jax.experimental.pallas import tpu as pltpu
from jax.sharding import PartitionSpec as P

MESH = pl.DeviceIdType.MESH
COUPLE, COL_E, COL_W, ROW_N, ROW_S, TOP_E, TOP_W, TOP_N, TOP_S = range(9)


def reversed_lanes(x, lane):
    width = x.shape[-1]
    bit = 1
    while bit < width:
        up = pltpu.roll(x, width - bit, x.ndim - 1)
        down = pltpu.roll(x, bit, x.ndim - 1)
        x = jnp.where((lane & bit) == 0, up, down)
        bit *= 2
    return x


def kernel(
    lats, lons, adj_h, mask_h, depth_h, weight_h, diff_h, vel_h, mix_h, out_h,
    field_a, field_b, diff, vel, mix, mask_i, depth, weight, vert,
    share, flux, col_out, col_w, col_e, top_col_out, top_col_w, top_col_e,
    north_out, south_out, north_in, south_in,
    top_north_out, top_south_out, top_north_in, top_south_in,
    load_sem, store_sem, send_sem, recv_sem,
):
    fields, levels, rows, cols = field_a.shape
    steps = diff.shape[0]
    chunk = store_sem.shape[0]
    span = levels // chunk
    ice, lat, lon = lax.axis_index("ice"), lax.axis_index("lat"), lax.axis_index("lon")
    partner = (1 - ice, lat, lon)
    east = (ice, lat, lax.rem(lon + 1, lons))
    west = (ice, lat, lax.rem(lon + lons - 1, lons))
    north = (ice, lat + 1, lon)
    south = (ice, lat - 1, lon)
    mirror = (ice, lat, lons - 1 - lon)
    top, bottom = lat == lats - 1, lat == 0

    loads = [
        pltpu.make_async_copy(depth_h.at[0], depth, load_sem.at[0]),
        pltpu.make_async_copy(weight_h.at[0], weight, load_sem.at[1]),
        pltpu.make_async_copy(mask_h, mask_i, load_sem.at[2]),
    ]
    for c in range(chunk):
        part = pl.ds(c * span, span)
        loads.append(pltpu.make_async_copy(adj_h.at[0, :, part], field_a.at[:, part], load_sem.at[3 + c]))
    coeffs = []
    for moment in range(steps):
        base = 3 + chunk + 3 * moment
        coeffs.append([
            pltpu.make_async_copy(diff_h.at[moment, 0], diff.at[moment], load_sem.at[base]),
            pltpu.make_async_copy(vel_h.at[moment, 0], vel.at[moment], load_sem.at[base + 1]),
            pltpu.make_async_copy(mix_h.at[moment, 0], mix.at[moment], load_sem.at[base + 2]),
        ])
    for copy in loads:
        copy.start()
    for moment in reversed(range(steps)):
        for copy in coeffs[moment]:
            copy.start()

    barrier = pltpu.get_barrier_semaphore()
    for peer in (partner, east, west):
        pl.semaphore_signal(barrier, inc=1, device_id=peer, device_id_type=MESH)

    @pl.when(top)
    def _():
        pl.semaphore_signal(barrier, inc=1, device_id=mirror, device_id_type=MESH)

    @pl.when(jnp.logical_not(top))
    def _():
        pl.semaphore_signal(barrier, inc=1, device_id=north, device_id_type=MESH)

    @pl.when(jnp.logical_not(bottom))
    def _():
        pl.semaphore_signal(barrier, inc=1, device_id=south, device_id_type=MESH)

    lane = lax.broadcasted_iota(jnp.int32, (rows, cols), 1)
    row = lax.broadcasted_iota(jnp.int32, (rows, cols), 0)
    lane8 = lax.broadcasted_iota(jnp.int32, (8, cols), 1)
    row8 = lax.broadcasted_iota(jnp.int32, (8, cols), 0)
    ends8 = jnp.logical_or(lane8 == 0, lane8 == cols - 1)
    for q in range(fields):
        vert[q, 0] = jnp.zeros((rows, cols), jnp.float32)
        vert[q, levels + 1] = jnp.zeros((rows, cols), jnp.float32)

    @pl.when(bottom)
    def _():
        south_in[...] = jnp.zeros_like(south_in)
        top_south_in[...] = jnp.zeros_like(top_south_in)

    def remote(step, which, src, dst, peer):
        return pltpu.make_async_remote_copy(
            src_ref=src, dst_ref=dst, send_sem=send_sem.at[step, which],
            recv_sem=recv_sem.at[step, which], device_id=peer, device_id_type=MESH,
        )

    def row_copies(step, which_n, which_s, n_out, s_out, n_in, s_in):
        return [
            (remote(step, which_s, n_out.at[step], s_in.at[step], north), jnp.logical_not(top)),
            (remote(step, which_n, n_out.at[step], n_in.at[step], mirror), top),
            (remote(step, which_n, s_out.at[step], n_in.at[step], south), jnp.logical_not(bottom)),
        ]

    def start_rows(copies):
        for copy, go in copies:
            pl.when(go)(copy.start)

    half = fields // 2

    def edges(step, moment, k, src, packed, place, put_rows):
        mask = mask_i[...].astype(jnp.float32)
        d, z = diff[moment, k] * mask, vel[moment, 0, k] * mask
        v = mix[moment, k] * mask
        both = d + jnp.where(lane == cols - 1, -z, z)
        last, first = slice(rows - 1, rows), slice(0, 1)
        b_last, b_first = vel[moment, 1, k, last] * mask[last], vel[moment, 1, k, first] * mask[first]
        to_north, to_south = d[last] - b_last, d[first] + b_first
        packed = list(packed)
        for q in range(fields):
            a = src[q, k]
            vert[q, k + 1] = v * a
            slot, spot = place(q)
            turned = pltpu.roll(both * a, 2 * spot + 1, 1)
            packed[slot] = jnp.where((lane >> 1) == spot, turned, packed[slot])
            put_rows(q, to_north * a[last], to_south * a[first])
        return tuple(packed)

    def interior(moment, k, src, dst):
        mask = mask_i[...].astype(jnp.float32)
        d, z, b = diff[moment, k] * mask, vel[moment, 0, k] * mask, vel[moment, 1, k] * mask
        own = mask - 4.0 * d - 2.0 * (mix[moment, k] * mask)
        eastward = jnp.where(lane == cols - 1, 0.0, d - z)
        westward = jnp.where(lane == 0, 0.0, d + z)
        northward = jnp.where(row == rows - 1, 0.0, d - b)
        southward = jnp.where(row == 0, 0.0, d + b)
        for q in range(fields):
            a = src[q, k]
            total = own * a + vert[q, k] + vert[q, k + 2]
            total = total + pltpu.roll(eastward * a, 1, 1) + pltpu.roll(westward * a, cols - 1, 1)
            total = total + pltpu.roll(northward * a, 1, 0) + pltpu.roll(southward * a, rows - 1, 0)
            dst[q, k] = total

    def finish(k, q, dst, packed, spot, from_south, from_north):
        parts = []
        for r in range(0, rows, 8):
            turned = pltpu.roll(packed[r:r + 8], cols - 1 - 2 * spot, 1)
            total = dst[q, k, r:r + 8] + jnp.where(ends8, turned, 0.0)
            if r == 0:
                total = total + jnp.where(row8 == 0, from_south, 0.0)
            if r == rows - 8:
                total = total + jnp.where(row8 == 7, from_north, 0.0)
            dst[q, k, r:r + 8] = total
            parts.append(total)
        return jnp.concatenate(parts, axis=0)

    def joined(from_west, from_east):
        return jnp.where(
            (lane & 1) == 1, pltpu.roll(from_west, 1, 1), pltpu.roll(from_east, cols - 1, 1)
        )

    loads[0].wait()
    zero = jnp.zeros((rows, cols), jnp.float32)
    sums = (zero,) * fields
    for c in range(chunk):
        loads[3 + c].wait()

        def add(k, sums):
            live = k < depth[...]
            return tuple(s + jnp.where(live, field_a[q, k], 0.0) for q, s in enumerate(sums))

        sums = lax.fori_loop(c * span, (c + 1) * span, add, sums)
    loads[1].wait()
    loads[2].wait()

    @pl.when(bottom)
    def _():
        pl.semaphore_wait(barrier, 4)

    @pl.when(jnp.logical_not(bottom))
    def _():
        pl.semaphore_wait(barrier, 5)

    pending = []
    stores = []
    for step in range(steps):
        moment = steps - 1 - step
        src, dst = (field_a, field_b) if step % 2 == 0 else (field_b, field_a)
        final = step == steps - 1
        scale = 1.0 / depth[...].astype(jnp.float32)
        for q in range(fields):
            share[step, q] = weight[q] * (scale * sums[q])
        couple = remote(step, COUPLE, share.at[step], flux.at[step], partner)
        couple.start()
        for copy in coeffs[moment]:
            copy.wait()

        for q in range(fields):
            north_out[step, q, 0:1] = jnp.zeros((1, cols), jnp.float32)
            south_out[step, q, 0:1] = jnp.zeros((1, cols), jnp.float32)

        def deep(k, packed):
            def put(q, up, down):
                north_out[step, q, pl.ds(k, 1)] = up
                south_out[step, q, pl.ds(k, 1)] = down

            return edges(
                step, moment, k, src, packed, lambda q: (q // half, (q % half) * levels + k), put
            )

        packed = lax.fori_loop(1, levels, deep, (zero, zero))
        for slot in range(2):
            col_out[step, slot] = packed[slot]
        send_e = remote(step, COL_E, col_out.at[step], col_w.at[step], east)
        send_w = remote(step, COL_W, col_out.at[step], col_e.at[step], west)
        send_rows = row_copies(step, ROW_N, ROW_S, north_out, south_out, north_in, south_in)
        start_rows(send_rows)
        send_e.start()
        send_w.start()

        couple.wait_recv()
        for q in range(fields):
            src[q, 0] = src[q, 0] + (flux[step, q] - share[step, q])

        def put_top(q, up, down):
            top_north_out[step, q:q + 1] = up
            top_south_out[step, q:q + 1] = down

        (top_packed,) = edges(step, moment, 0, src, (zero,), lambda q: (0, q), put_top)
        top_col_out[step] = top_packed
        top_e = remote(step, TOP_E, top_col_out.at[step], top_col_w.at[step], east)
        top_w = remote(step, TOP_W, top_col_out.at[step], top_col_e.at[step], west)
        top_rows = row_copies(
            step, TOP_N, TOP_S, top_north_out, top_south_out, top_north_in, top_south_in
        )
        start_rows(top_rows)
        top_e.start()
        top_w.start()

        def inner(k, carry):
            interior(moment, k, src, dst)
            return carry

        lax.fori_loop(0, levels, inner, 0)

        for copy in (send_e, send_w, top_e, top_w):
            copy.wait_recv()
        for copies in (send_rows, top_rows):
            copies[1][0].wait_recv()
            pl.when(jnp.logical_not(bottom))(copies[0][0].wait_recv)

        @pl.when(top)
        def _():
            lane_s = lax.broadcasted_iota(jnp.int32, (levels, cols), 1)
            for q in range(fields):
                turned = reversed_lanes(north_in[step, q], lane_s)
                north_in[step, q] = turned if q < half else -turned
            lane_f = lax.broadcasted_iota(jnp.int32, (fields, cols), 1)
            sign = lax.broadcasted_iota(jnp.int32, (fields, cols), 0)
            turned = reversed_lanes(top_north_in[step], lane_f)
            top_north_in[step] = jnp.where(sign < half, turned, -turned)

        pair = [joined(col_w[step, slot], col_e[step, slot]) for slot in range(2)]
        top_pair = joined(top_col_w[step], top_col_e[step])
        sums = []
        for q in range(fields):
            total = finish(
                0, q, dst, top_pair, q,
                top_south_in[step, q:q + 1], top_north_in[step, q:q + 1],
            )
            sums.append(total)
        sums = tuple(sums)
        for c in range(chunk):

            def last(k, sums):
                out = []
                for q in range(fields):
                    total = finish(
                        k, q, dst, pair[q // half], (q % half) * levels + k,
                        south_in[step, q, pl.ds(k, 1)], north_in[step, q, pl.ds(k, 1)],
                    )
                    if not final:
                        out.append(sums[q] + jnp.where(k < depth[...], total, 0.0))
                return tuple(out) if not final else sums

            lower = max(1, c * span)
            sums = lax.fori_loop(lower, (c + 1) * span, last, sums if not final else 0)
            if final:
                part = pl.ds(c * span, span)
                copy = pltpu.make_async_copy(dst.at[:, part], out_h.at[0, :, part], store_sem.at[c])
                copy.start()
                stores.append(copy)

        pending += [(couple, None), (send_e, None), (send_w, None), (top_e, None), (top_w, None)]
        pending += send_rows + top_rows

    for copy, go in pending:
        if go is None:
            copy.wait_send()
        else:
            pl.when(go)(copy.wait_send)
    for copy in stores:
        copy.wait()


def solution(mesh):
    lats, lons = mesh.shape["lat"], mesh.shape["lon"]

    def shards(adjoint, land_mask, coupling_depth, coupling_weight, diffusion, velocity, mixing):
        _, fields, levels, rows, cols = adjoint.shape
        steps = diffusion.shape[0]
        chunk = 3
        f32 = jnp.float32
        block = (rows, cols)
        column = pltpu.VMEM((steps, 2, rows, cols), f32)
        top_column = pltpu.VMEM((steps, rows, cols), f32)
        edge = pltpu.VMEM((steps, fields, levels, cols), f32)
        top_edge = pltpu.VMEM((steps, fields, cols), f32)
        return pl.pallas_call(
            functools.partial(kernel, lats, lons),
            out_shape=jax.ShapeDtypeStruct(adjoint.shape, f32),
            in_specs=[pl.BlockSpec(memory_space=pl.ANY)] * 7,
            out_specs=pl.BlockSpec(memory_space=pl.ANY),
            scratch_shapes=[
                pltpu.VMEM((fields, levels, rows, cols), f32),
                pltpu.VMEM((fields, levels, rows, cols), f32),
                pltpu.VMEM((steps, levels, rows, cols), f32),
                pltpu.VMEM((steps, 2, levels, rows, cols), f32),
                pltpu.VMEM((steps, levels, rows, cols), f32),
                pltpu.VMEM(block, jnp.int32),
                pltpu.VMEM(block, jnp.int32),
                pltpu.VMEM((fields, rows, cols), f32),
                pltpu.VMEM((fields, levels + 2, rows, cols), f32),
                pltpu.VMEM((steps, fields, rows, cols), f32),
                pltpu.VMEM((steps, fields, rows, cols), f32),
                column, column, column,
                top_column, top_column, top_column,
                edge, edge, edge, edge,
                top_edge, top_edge, top_edge, top_edge,
                pltpu.SemaphoreType.DMA((3 + chunk + 3 * steps,)),
                pltpu.SemaphoreType.DMA((chunk,)),
                pltpu.SemaphoreType.DMA((steps, 12)),
                pltpu.SemaphoreType.DMA((steps, 9)),
            ],
            compiler_params=pltpu.CompilerParams(
                collective_id=0, has_side_effects=True, vmem_limit_bytes=60 * 1024 * 1024
            ),
            name="adjoint",
        )(adjoint, land_mask, coupling_depth, coupling_weight, diffusion, velocity, mixing)

    in_specs = (
        P("ice", None, None, "lat", "lon"),
        P("lat", "lon"),
        P("ice", "lat", "lon"),
        P("ice", None, "lat", "lon"),
        P(None, "ice", None, "lat", "lon"),
        P(None, "ice", None, None, "lat", "lon"),
        P(None, "ice", None, "lat", "lon"),
    )
    out_specs = P("ice", None, None, "lat", "lon")
    return jax.shard_map(shards, mesh=mesh, in_specs=in_specs, out_specs=out_specs, check_vma=False)
```

time: 150 us -> 27.9 us (0.19)
  the two profiles are of different devices: /device:TPU:12 before, /device:TPU:6 now
where the time goes in v1:
time: 27.9 us; the launch traced here: 27.7 us
  Pallas kernels  25 us (90%)
  local copies, waits for them, and re-layouts  2.67 us (10%)
    pallas_call x1, Pallas kernels, shards(): pl.pallas_call(functools.partial(kernel, lats, lons), out_shape=jax.Shape...  25 us
    unnamed x1, local copies, waits for them, and re-layouts  2.67 us

profile of v1, /device:TPU:6, one launch (start us, length us, event | category | flops | bytes accessed | tf_op | source)
XLA Modules:
  0.0 27.7 jit_solution(9016896970015734035)
XLA Ops:
  0.0 25.0 %adjoint.1 = f32[1,4,24,32,128]{4,3,2,1,0:T(8,128)} custom-call(f32[1,4,24,32,128]{4,3,2,1,0:T(8,128)} %adj_h.1, s32[32,128]{1,0:T(8,128)} %mask_h.1, s32[1,32,128]{2,1,0:T(8,128)} %depth_h.1, f32[1,4,32,128]{3,2,1,0:T(8,128)} %weight_h.1, f32[2,1,24,32,128]{4,3,2,1,0:T(8,128)} %diff_h.1, f32[2,1,2,24,32,128]{5,4,3,2,1,0:T(8,128)} %vel_h.1, ...), custom_call_target="tpu_custom_call" | custom-call | tf_op jit(solution)/shard_map/adjoint/pallas_call | solution.py:325
  25.0 2.7 %copy.9 = f32[1,4,24,32,128]{4,3,2,1,0:T(8,128)} copy(f32[1,4,24,32,128]{4,3,2,1,0:T(8,128)} %adjoint.1) | data formatting | bytes 3145728

commit v2 on v1

--- a/solution.py
+++ b/solution.py
@@ -8,7 +8,23 @@
 from jax.sharding import PartitionSpec as P
 
 MESH = pl.DeviceIdType.MESH
+EDGE, INNER, LAST = 8, 4, 8
 COUPLE, COL_E, COL_W, ROW_N, ROW_S, TOP_E, TOP_W, TOP_N, TOP_S = range(9)
+
+
+def levels_loop(lower, upper, body, carry, times):
+    whole = (upper - lower) // times
+
+    def some(i, carry):
+        for j in range(times):
+            carry = body(lower + i * times + j, carry)
+        return carry
+
+    if whole > 0:
+        carry = lax.fori_loop(0, whole, some, carry)
+    for k in range(lower + whole * times, upper):
+        carry = body(k, carry)
+    return carry
 
 
 def reversed_lanes(x, lane):
@@ -175,7 +191,7 @@
             live = k < depth[...]
             return tuple(s + jnp.where(live, field_a[q, k], 0.0) for q, s in enumerate(sums))
 
-        sums = lax.fori_loop(c * span, (c + 1) * span, add, sums)
+        sums = levels_loop(c * span, (c + 1) * span, add, sums, 4)
     loads[1].wait()
     loads[2].wait()
 
@@ -214,7 +230,7 @@
                 step, moment, k, src, packed, lambda q: (q // half, (q % half) * levels + k), put
             )
 
-        packed = lax.fori_loop(1, levels, deep, (zero, zero))
+        packed = levels_loop(1, levels, deep, (zero, zero), EDGE)
         for slot in range(2):
             col_out[step, slot] = packed[slot]
         send_e = remote(step, COL_E, col_out.at[step], col_w.at[step], east)
@@ -247,7 +263,7 @@
             interior(moment, k, src, dst)
             return carry
 
-        lax.fori_loop(0, levels, inner, 0)
+        levels_loop(0, levels, inner, 0, INNER)
 
         for copy in (send_e, send_w, top_e, top_w):
             copy.wait_recv()
@@ -290,7 +306,7 @@
                 return tuple(out) if not final else sums
 
             lower = max(1, c * span)
-            sums = lax.fori_loop(lower, (c + 1) * span, last, sums if not final else 0)
+            sums = levels_loop(lower, (c + 1) * span, last, sums if not final else 0, LAST)
             if final:
                 part = pl.ds(c * span, span)
                 copy = pltpu.make_async_copy(dst.at[:, part], out_h.at[0, :, part], store_sem.at[c])

time: 27.9 us -> 22.2 us (0.80)
  Pallas kernels: 25 us -> 19.2 us
    pallas_call x1, Pallas kernels: 25 us -> 19.2 us  [shards(): pl.pallas_call(functools.partial(kernel, lats, lons), out_shape=jax.Shape...]
where the time goes in v2:
time: 22.2 us; the launch traced here: 21.9 us
  Pallas kernels  19.2 us (86%)
  local copies, waits for them, and re-layouts  2.67 us (12%)
    pallas_call x1, Pallas kernels, shards(): pl.pallas_call(functools.partial(kernel, lats, lons), out_shape=jax.Shape...  19.2 us
    unnamed x1, local copies, waits for them, and re-layouts  2.67 us

profile of v2, /device:TPU:6, one launch (start us, length us, event | category | flops | bytes accessed | tf_op | source)
XLA Modules:
  0.0 21.9 jit_solution(524040850369283859)
XLA Ops:
  0.0 19.2 %adjoint.1 = f32[1,4,24,32,128]{4,3,2,1,0:T(8,128)} custom-call(f32[1,4,24,32,128]{4,3,2,1,0:T(8,128)} %adj_h.1, s32[32,128]{1,0:T(8,128)} %mask_h.1, s32[1,32,128]{2,1,0:T(8,128)} %depth_h.1, f32[1,4,32,128]{3,2,1,0:T(8,128)} %weight_h.1, f32[2,1,24,32,128]{4,3,2,1,0:T(8,128)} %diff_h.1, f32[2,1,2,24,32,128]{5,4,3,2,1,0:T(8,128)} %vel_h.1, ...), custom_call_target="tpu_custom_call" | custom-call | tf_op jit(solution)/shard_map/adjoint/pallas_call | solution.py:341
  19.3 2.7 %copy.9 = f32[1,4,24,32,128]{4,3,2,1,0:T(8,128)} copy(f32[1,4,24,32,128]{4,3,2,1,0:T(8,128)} %adjoint.1) | data formatting | bytes 3145728

commit v3 on v2

--- a/solution.py
+++ b/solution.py
@@ -209,6 +209,8 @@
         moment = steps - 1 - step
         src, dst = (field_a, field_b) if step % 2 == 0 else (field_b, field_a)
         final = step == steps - 1
+        if final:
+            dst = out_h.at[0]
         scale = 1.0 / depth[...].astype(jnp.float32)
         for q in range(fields):
             share[step, q] = weight[q] * (scale * sums[q])
@@ -307,11 +309,6 @@
 
             lower = max(1, c * span)
             sums = levels_loop(lower, (c + 1) * span, last, sums if not final else 0, LAST)
-            if final:
-                part = pl.ds(c * span, span)
-                copy = pltpu.make_async_copy(dst.at[:, part], out_h.at[0, :, part], store_sem.at[c])
-                copy.start()
-                stores.append(copy)
 
         pending += [(couple, None), (send_e, None), (send_w, None), (top_e, None), (top_w, None)]
         pending += send_rows + top_rows
@@ -341,8 +338,8 @@
         return pl.pallas_call(
             functools.partial(kernel, lats, lons),
             out_shape=jax.ShapeDtypeStruct(adjoint.shape, f32),
-            in_specs=[pl.BlockSpec(memory_space=pl.ANY)] * 7,
-            out_specs=pl.BlockSpec(memory_space=pl.ANY),
+            in_specs=[pl.BlockSpec(memory_space=pltpu.HBM)] * 7,
+            out_specs=pl.BlockSpec(memory_space=pltpu.VMEM),
             scratch_shapes=[
                 pltpu.VMEM((fields, levels, rows, cols), f32),
                 pltpu.VMEM((fields, levels, rows, cols), f32),
@@ -365,10 +362,10 @@
                 pltpu.SemaphoreType.DMA((steps, 9)),
             ],
             compiler_params=pltpu.CompilerParams(
-                collective_id=0, has_side_effects=True, vmem_limit_bytes=60 * 1024 * 1024
+                collective_id=0, has_side_effects=True, vmem_limit_bytes=40 * 1024 * 1024
             ),
             name="adjoint",
-        )(adjoint, land_mask, coupling_depth, coupling_weight, diffusion, velocity, mixing)
+        )(*(pltpu.with_memory_space_constraint(x, pltpu.HBM) for x in (adjoint, land_mask, coupling_depth, coupling_weight, diffusion, velocity, mixing)))
 
     in_specs = (
         P("ice", None, None, "lat", "lon"),

time: 22.2 us -> 19.8 us (0.89)
  local copies, waits for them, and re-layouts: 2.67 us -> 1.15 us
  Pallas kernels: 19.2 us -> 18.4 us
    unnamed x1, local copies, waits for them, and re-layouts: 2.67 us -> 1.15 us
    pallas_call x1, Pallas kernels: 19.2 us -> 18.4 us  [shards(): pl.pallas_call(functools.partial(kernel, lats, lons), out_shape=jax.Shape...]
where the time goes in v3:
time: 19.8 us; the launch traced here: 19.5 us
  Pallas kernels  18.4 us (93%)
  local copies, waits for them, and re-layouts  1.15 us (6%)
    pallas_call x1, Pallas kernels, shards(): pl.pallas_call(functools.partial(kernel, lats, lons), out_shape=jax.Shape...  18.4 us
    unnamed x1, local copies, waits for them, and re-layouts  1.15 us

profile of v3, /device:TPU:6, one launch (start us, length us, event | category | flops | bytes accessed | tf_op | source)
XLA Modules:
  0.0 19.5 jit_solution(7048260398408182930)
XLA Ops:
  0.0 18.4 %adjoint.1 = f32[1,4,24,32,128]{4,3,2,1,0:T(8,128)S(1)} custom-call(f32[1,4,24,32,128]{4,3,2,1,0:T(8,128)} %adj_h.1, s32[32,128]{1,0:T(8,128)} %mask_h.1, s32[1,32,128]{2,1,0:T(8,128)} %depth_h.1, f32[1,4,32,128]{3,2,1,0:T(8,128)} %weight_h.1, f32[2,1,24,32,128]{4,3,2,1,0:T(8,128)} %diff_h.1, f32[2,1,2,24,32,128]{5,4,3,2,1,0:T(8,128)} %vel_h.1, ...), custom_call_target="tpu_custom_call" | custom-call | tf_op jit(solution)/shard_map/adjoint/pallas_call | solution.py:338
  18.4 1.1 %copy.9 = f32[1,4,24,32,128]{4,3,2,1,0:T(8,128)} copy(f32[1,4,24,32,128]{4,3,2,1,0:T(8,128)S(1)} %adjoint.1) | data formatting | bytes 3145728

commit v4 on v3

--- a/solution.py
+++ b/solution.py
@@ -117,11 +117,12 @@
             recv_sem=recv_sem.at[step, which], device_id=peer, device_id_type=MESH,
         )
 
-    def row_copies(step, which_n, which_s, n_out, s_out, n_in, s_in):
+    def row_copies(step, which_n, which_s, n_out, s_out, n_in, s_in, part=()):
+        at = (step,) + part
         return [
-            (remote(step, which_s, n_out.at[step], s_in.at[step], north), jnp.logical_not(top)),
-            (remote(step, which_n, n_out.at[step], n_in.at[step], mirror), top),
-            (remote(step, which_n, s_out.at[step], n_in.at[step], south), jnp.logical_not(bottom)),
+            (remote(step, which_s, n_out.at[at], s_in.at[at], north), jnp.logical_not(top)),
+            (remote(step, which_n, n_out.at[at], n_in.at[at], mirror), top),
+            (remote(step, which_n, s_out.at[at], n_in.at[at], south), jnp.logical_not(bottom)),
         ]
 
     def start_rows(copies):
@@ -176,10 +177,12 @@
             parts.append(total)
         return jnp.concatenate(parts, axis=0)
 
-    def joined(from_west, from_east):
-        return jnp.where(
-            (lane & 1) == 1, pltpu.roll(from_west, 1, 1), pltpu.roll(from_east, cols - 1, 1)
-        )
+    def joined(from_west, from_east, turn_west, turn_east):
+        if turn_west:
+            from_west = pltpu.roll(from_west, turn_west, 1)
+        if turn_east:
+            from_east = pltpu.roll(from_east, turn_east, 1)
+        return jnp.where((lane & 1) == 1, from_west, from_east)
 
     loads[0].wait()
     zero = jnp.zeros((rows, cols), jnp.float32)
@@ -232,13 +235,21 @@
                 step, moment, k, src, packed, lambda q: (q // half, (q % half) * levels + k), put
             )
 
-        packed = levels_loop(1, levels, deep, (zero, zero), EDGE)
-        for slot in range(2):
-            col_out[step, slot] = packed[slot]
-        send_e = remote(step, COL_E, col_out.at[step], col_w.at[step], east)
-        send_w = remote(step, COL_W, col_out.at[step], col_e.at[step], west)
-        send_rows = row_copies(step, ROW_N, ROW_S, north_out, south_out, north_in, south_in)
-        start_rows(send_rows)
+        packed = (zero, zero)
+        groups = []
+        for c in range(chunk):
+            packed = levels_loop(max(1, c * span), (c + 1) * span, deep, packed, EDGE)
+            part = pl.ds(c * span, span)
+            which_n, which_s = (ROW_N, ROW_S) if c == 0 else (7 + 2 * c, 8 + 2 * c)
+            groups.append(row_copies(
+                step, which_n, which_s, north_out, south_out, north_in, south_in, (slice(None), part)
+            ))
+            start_rows(groups[-1])
+        odd = (lane & 1) == 1
+        col_out[step, 0] = jnp.where(odd, pltpu.roll(packed[1], 1, 1), packed[0])
+        col_out[step, 1] = jnp.where(odd, packed[1], pltpu.roll(packed[0], cols - 1, 1))
+        send_e = remote(step, COL_E, col_out.at[step, 0], col_w.at[step], east)
+        send_w = remote(step, COL_W, col_out.at[step, 1], col_e.at[step], west)
         send_e.start()
         send_w.start()
 
@@ -269,7 +280,7 @@
 
         for copy in (send_e, send_w, top_e, top_w):
             copy.wait_recv()
-        for copies in (send_rows, top_rows):
+        for copies in groups + [top_rows]:
             copies[1][0].wait_recv()
             pl.when(jnp.logical_not(bottom))(copies[0][0].wait_recv)
 
@@ -284,8 +295,10 @@
             turned = reversed_lanes(top_north_in[step], lane_f)
             top_north_in[step] = jnp.where(sign < half, turned, -turned)
 
-        pair = [joined(col_w[step, slot], col_e[step, slot]) for slot in range(2)]
-        top_pair = joined(top_col_w[step], top_col_e[step])
+        pair = [
+            joined(col_w[step], col_e[step], 1, 0), joined(col_w[step], col_e[step], 0, cols - 1)
+        ]
+        top_pair = joined(top_col_w[step], top_col_e[step], 1, cols - 1)
         sums = []
         for q in range(fields):
             total = finish(
@@ -311,7 +324,8 @@
             sums = levels_loop(lower, (c + 1) * span, last, sums if not final else 0, LAST)
 
         pending += [(couple, None), (send_e, None), (send_w, None), (top_e, None), (top_w, None)]
-        pending += send_rows + top_rows
+        for copies in groups + [top_rows]:
+            pending += copies
 
     for copy, go in pending:
         if go is None:
@@ -352,14 +366,14 @@
                 pltpu.VMEM((fields, levels + 2, rows, cols), f32),
                 pltpu.VMEM((steps, fields, rows, cols), f32),
                 pltpu.VMEM((steps, fields, rows, cols), f32),
-                column, column, column,
+                column, top_column, top_column,
                 top_column, top_column, top_column,
                 edge, edge, edge, edge,
                 top_edge, top_edge, top_edge, top_edge,
                 pltpu.SemaphoreType.DMA((3 + chunk + 3 * steps,)),
                 pltpu.SemaphoreType.DMA((chunk,)),
-                pltpu.SemaphoreType.DMA((steps, 12)),
-                pltpu.SemaphoreType.DMA((steps, 9)),
+                pltpu.SemaphoreType.DMA((steps, 7 + 2 * chunk)),
+                pltpu.SemaphoreType.DMA((steps, 7 + 2 * chunk)),
             ],
             compiler_params=pltpu.CompilerParams(
                 collective_id=0, has_side_effects=True, vmem_limit_bytes=40 * 1024 * 1024

time: 19.8 us -> 18.5 us (0.934)
  Pallas kernels: 18.4 us -> 17.1 us
    pallas_call x1, Pallas kernels: 18.4 us -> 17.1 us  [shards(): pl.pallas_call(functools.partial(kernel, lats, lons), out_shape=jax.Shape...]
where the time goes in v4:
time: 18.5 us; the launch traced here: 18.2 us
  Pallas kernels  17.1 us (92%)
  local copies, waits for them, and re-layouts  1.15 us (6%)
    pallas_call x1, Pallas kernels, shards(): pl.pallas_call(functools.partial(kernel, lats, lons), out_shape=jax.Shape...  17.1 us
    unnamed x1, local copies, waits for them, and re-layouts  1.15 us

profile of v4, /device:TPU:6, one launch (start us, length us, event | category | flops | bytes accessed | tf_op | source)
XLA Modules:
  0.0 18.2 jit_solution(11592251319749913081)
XLA Ops:
  0.0 17.1 %adjoint.1 = f32[1,4,24,32,128]{4,3,2,1,0:T(8,128)S(1)} custom-call(f32[1,4,24,32,128]{4,3,2,1,0:T(8,128)} %adj_h.1, s32[32,128]{1,0:T(8,128)} %mask_h.1, s32[1,32,128]{2,1,0:T(8,128)} %depth_h.1, f32[1,4,32,128]{3,2,1,0:T(8,128)} %weight_h.1, f32[2,1,24,32,128]{4,3,2,1,0:T(8,128)} %diff_h.1, f32[2,1,2,24,32,128]{5,4,3,2,1,0:T(8,128)} %vel_h.1, ...), custom_call_target="tpu_custom_call" | custom-call | tf_op jit(solution)/shard_map/adjoint/pallas_call | solution.py:352
  17.1 1.1 %copy.9 = f32[1,4,24,32,128]{4,3,2,1,0:T(8,128)} copy(f32[1,4,24,32,128]{4,3,2,1,0:T(8,128)S(1)} %adjoint.1) | data formatting | bytes 3145728
